TPU v7x, 32 devices: a whole 2x2x4 slice. The times are simulated.
32 devices in a mesh: col: 4 (over y, x), bulk: 8 (over z, core).
Axes of the slice: x: 2, y: 2, z: 4, core: 2. Of those that a mesh axis runs over, the one named last changes fastest.
Arguments:
- sequence_embedding: bfloat16 [64, 128, 64], P('bulk', 'col'), may hold values from -6 to 6
- residue_couplings: bfloat16 [128, 128, 128], P('bulk', 'col'), may hold values from -6 to 6
- sequence_layernorm_factor: float32 [64], replicated, may hold values from 0.5 to 1.5
- coupling_layernorm_factor: float32 [128], replicated, may hold values from 0.5 to 1.5
- content_projection: bfloat16 [64, 256], replicated, may hold values from -0.75 to 0.75
- switch_projection: bfloat16 [64, 256], replicated, may hold values from -0.75 to 0.75
- attention_score_projection: bfloat16 [128, 8], replicated, may hold values from -0.29882812 to 0.29882812
- final_projection: bfloat16 [256, 64], replicated, may hold values from -2 to 2
- residual_change_cotangent: bfloat16 [64, 128, 64], P('bulk', 'col'), may hold values from -6 to 6
Outputs:
- residual_change: bfloat16 [64, 128, 64], P('bulk', 'col')
- sequence_embedding_sensitivity: bfloat16 [64, 128, 64], P('bulk', 'col')
- coupling_sensitivity: bfloat16 [128, 128, 128], P('bulk', 'col')
All inputs are finite; a program needn't handle non-finite values.
Results may differ from a plain program's by a relative error of at most 0.025.
Values may be sent and summed in bfloat16 or wider, within the bound.
A program may use at most 64 MiB of HBM per device.

v0:
```python
import jax
import jax.numpy as jnp
from jax import lax
from jax.sharding import PartitionSpec as P

epsilon = 1e-05


def centred_sequences(inputs, scale_gain):
    widened = inputs.astype(jnp.float32)
    row_mean = jnp.mean(widened, axis=-1, keepdims=True)
    centered = widened - row_mean
    variance = jnp.mean(centered * centered, axis=-1, keepdims=True)
    inv_std = lax.rsqrt(variance + epsilon)
    normed = centered * inv_std
    return (normed * scale_gain, normed, inv_std)


def layernorm_reverse_mode(upstream, normed, inv_std, scale_gain):
    scaled = upstream * scale_gain
    mean_grad = jnp.mean(scaled, axis=-1, keepdims=True)
    mean_proj = jnp.mean(scaled * normed, axis=-1, keepdims=True)
    return inv_std * (scaled - mean_grad - normed * mean_proj)


def per_device(
    sequence_embedding,
    residue_couplings,
    sequence_layernorm_factor,
    coupling_layernorm_factor,
    content_projection,
    switch_projection,
    attention_score_projection,
    final_projection,
    residual_change_cotangent,
):
    number_of_heads = attention_score_projection.shape[1]
    value_channels = content_projection.shape[1]
    head_channels = value_channels // number_of_heads
    device_sequences = sequence_embedding.shape[0]
    device_residues = sequence_embedding.shape[1]
    finest_accuracy = lax.Precision.HIGHEST
    out_wide = final_projection.astype(jnp.float32)
    switch_single_form = switch_projection.astype(jnp.float32)
    bias_wide = attention_score_projection.astype(jnp.float32)
    pair_scaled, pair_hat, pair_inv = centred_sequences(
        residue_couplings, coupling_layernorm_factor
    )
    logits = jnp.einsum(
        "ijk,kh->hij",
        pair_scaled.astype(jnp.bfloat16),
        attention_score_projection,
        preferred_element_type=jnp.float32,
    )
    exponent = jnp.exp(logits)
    totals = lax.psum(jnp.sum(exponent, axis=2), "col")
    weights = exponent / totals[:, :, None]
    weights_low = weights.astype(jnp.bfloat16)
    weight_panel = lax.all_gather(weights_low, "bulk", axis=1, tiled=True)
    all_tokens = weight_panel.shape[1]
    sequence_scaled_by_factor, sequence_centred_unit, sequence_reciprocal_spread = (
        centred_sequences(sequence_embedding, sequence_layernorm_factor)
    )
    sequence_embedding_brief = sequence_scaled_by_factor.astype(jnp.bfloat16)
    content_sequences = jnp.dot(
        sequence_embedding_brief, content_projection, preferred_element_type=jnp.float32
    ).astype(jnp.bfloat16)
    value_per_head = content_sequences.reshape(
        device_sequences, device_residues, number_of_heads, head_channels
    )
    partial_value = jnp.einsum(
        "hij,sjhc->sihc", weight_panel, value_per_head, preferred_element_type=jnp.float32
    ).reshape(device_sequences, all_tokens, value_channels)
    partial_low = partial_value.astype(jnp.bfloat16)
    sigmoid_switch = jax.nn.sigmoid(
        jnp.dot(sequence_embedding_brief, switch_projection, preferred_element_type=jnp.float32)
    )
    pair_average = lax.psum_scatter(partial_low, "col", scatter_dimension=1, tiled=True).astype(
        jnp.float32
    )
    residual_change = jnp.dot(
        sigmoid_switch * pair_average, out_wide, precision=finest_accuracy
    ).astype(jnp.bfloat16)
    d_gated = jnp.dot(
        residual_change_cotangent.astype(jnp.float32), out_wide.T, precision=finest_accuracy
    )
    d_average_here = (sigmoid_switch * d_gated).astype(jnp.bfloat16)
    average_gradient = lax.all_gather(d_average_here, "col", axis=1, tiled=True)
    switch_preimage_sensitivity = d_gated * pair_average * sigmoid_switch * (1.0 - sigmoid_switch)
    gate_contribution = jnp.dot(
        switch_preimage_sensitivity, switch_single_form.T, precision=finest_accuracy
    )
    head_gradient = average_gradient.reshape(
        device_sequences, all_tokens, number_of_heads, head_channels
    )
    content_sensitivity = jnp.einsum(
        "hij,sihc->sjhc", weight_panel, head_gradient, preferred_element_type=jnp.float32
    )
    content_sensitivity = content_sensitivity.reshape(
        device_sequences, device_residues, value_channels
    ).astype(jnp.bfloat16)
    weight_part = jnp.einsum(
        "sihc,sjhc->hij", head_gradient, value_per_head, preferred_element_type=jnp.float32
    )
    d_weights = lax.psum_scatter(
        weight_part.astype(jnp.bfloat16), "bulk", scatter_dimension=1, tiled=True
    ).astype(jnp.float32)
    row_dot = lax.psum(jnp.sum(weights_low.astype(jnp.float32) * d_weights, axis=2), "col")
    d_logits = weights * (d_weights - row_dot[:, :, None])
    d_pair_low = jnp.einsum("hij,kh->ijk", d_logits, bias_wide, precision=finest_accuracy)
    coupling_sensitivity = layernorm_reverse_mode(
        d_pair_low, pair_hat, pair_inv, coupling_layernorm_factor
    ).astype(jnp.bfloat16)
    sequence_sensitivity_brief = (
        jnp.dot(content_sensitivity, content_projection.T, preferred_element_type=jnp.float32)
        + gate_contribution
    )
    sequence_embedding_sensitivity = layernorm_reverse_mode(
        sequence_sensitivity_brief,
        sequence_centred_unit,
        sequence_reciprocal_spread,
        sequence_layernorm_factor,
    ).astype(jnp.bfloat16)
    return (residual_change, sequence_embedding_sensitivity, coupling_sensitivity)


def solution(mesh):
    in_specs = (
        P("bulk", "col", None),
        P("bulk", "col", None),
        P(),
        P(),
        P(),
        P(),
        P(),
        P(),
        P("bulk", "col", None),
    )
    out_specs = (P("bulk", "col", None), P("bulk", "col", None), P("bulk", "col", None))
    return jax.shard_map(
        per_device, mesh=mesh, in_specs=in_specs, out_specs=out_specs, check_vma=False
    )
```

profile of v0, /device:TPU:0, one launch (start us, length us, event | category | flops | bytes accessed | tf_op | source)
XLA Modules:
  0.0 105.6 jit_solution(678878752773036502)
XLA Ops:
  7.2 0.0 copy-start
  7.2 0.0 copy-start.1
  7.2 0.0 reduce-scatter.5.cloned.1.call-start
  7.2 1.0 convert_reduce_fusion.1
  8.2 0.0 copy-done.1
  8.2 0.0 copy-start.4
  8.2 0.2 fusion.39
  8.4 0.0 copy-start.8
  8.5 0.5 copy-done.4
  9.0 0.1 copy-done.8
  9.1 0.2 convolution_convert_fusion.2
  9.4 0.0 copy-start.5
  9.4 0.2 reshape.60
  9.6 0.0 copy-done
  9.6 0.5 copy-done.5
  10.1 0.0 copy-start.6
  10.1 0.2 fusion.50
  10.3 0.6 copy-done.6
  10.9 0.3 multiply_convert_fusion
  11.2 11.5 %all_gather.7 = bf16[8,128,256]{2,1,0:T(8,128)(2,1)S(1)} all-gather(bf16[8,32,256]{2,1,0:T(8,128)(2,1)S(1)} %get-tuple-element.9), channel_id=1, replica_groups=mesh['col'=4,'bulk'=8] {'col'}, dimensions={1}, use_global_device_ids=true | all-gather | bytes 655360 | tf_op jit(solution)/shard_map/all_gather | solution.py:88
  22.7 0.3 copy.58
  23.0 0.3 fusion.6
  23.3 0.9 copy.64
  24.2 0.0 copy-start.2
  24.2 0.0 reduce-scatter.5.cloned.1.call-update
  24.2 0.0 reduce-scatter.3.cloned.1.call-start
  24.3 0.8 copy-done.2
  25.1 0.1 convert_reduce_fusion
  25.2 0.3 fusion.21
  25.5 0.0 copy-start.9
  25.5 0.0 copy-start.10
  25.5 0.6 copy-done.9
  26.2 0.0 copy-done.10
  26.2 0.4 fusion.65
  26.6 9.1 %psum.14 = f32[8,16]{0,1:T(8,128)S(1)} all-reduce(f32[8,16]{0,1:T(8,128)S(1)} %get-tuple-element.11), channel_id=1, replica_groups=mesh['col'=4,'bulk'=8] {'col'}, use_global_device_ids=true, to_apply=%region_5.0 | all-reduce | flops 128 | bytes 1024 | tf_op jit(solution)/shard_map/psum | solution.py:56
  35.7 19.7 %reduce-scatter.5.cloned.1.call-done = bf16[8,16,32]{2,0,1:T(8,128)(2,1)} async-done(((bf16[8,128,32]{2,0,1:T(8,128)(2,1)}), bf16[8,16,32]{2,0,1:T(8,128)(2,1)}) %reduce-scatter.5.cloned.1.call-update) | async-done | bytes 8208 | tf_op jit(solution)/shard_map/reduce_scatter | solution.py:105
  55.4 0.9 fusion.45
  56.3 14.2 %all_gather.6 = bf16[8,128,32]{2,0,1:T(8,128)(2,1)S(1)} all-gather(bf16[8,16,32]{2,0,1:T(8,128)(2,1)S(1)} %get-tuple-element.8), channel_id=1, replica_groups=mesh['col'=4,'bulk'=8] {'bulk'}, dimensions={1}, use_global_device_ids=true | all-gather | bytes 73728 | tf_op jit(solution)/shard_map/all_gather | solution.py:59
  70.5 0.4 fusion
  70.9 1.0 copy.57
  71.9 0.0 reduce-scatter.3.cloned.1.call-update
  71.9 0.3 fusion.1
  72.2 0.3 copy.61
  72.6 0.0 copy-start.7
  72.6 0.4 convert_element_type.78
  73.0 10.5 %psum.15 = f32[8,16]{0,1:T(8,128)S(1)} all-reduce(f32[8,16]{0,1:T(8,128)S(1)} %get-tuple-element.7), channel_id=1, replica_groups=mesh['col'=4,'bulk'=8] {'col'}, use_global_device_ids=true, to_apply=%region_11.0 | all-reduce | flops 128 | bytes 1024 | tf_op jit(solution)/shard_map/psum | solution.py:108
  83.4 0.0 copy-done.7
  83.4 0.7 fusion.62
  84.1 1.0 fusion.20
  85.1 10.4 %reduce-scatter.3.cloned.1.call-done = bf16[8,32,256]{2,1,0:T(8,128)(2,1)} async-done(((bf16[8,128,256]{2,1,0:T(8,128)(2,1)}), bf16[8,32,256]{2,1,0:T(8,128)(2,1)}) %reduce-scatter.3.cloned.1.call-update) | async-done | bytes 131088 | tf_op jit(solution)/shard_map/reduce_scatter | solution.py:78
  95.5 1.2 %fusion.24 = f32[8,32,64]{2,1,0:T(8,128)S(1)} fusion(f32[8,32,256]{2,1,0:T(8,128)S(1)} %get-tuple-element.10, f32[8,32,256]{2,1,0:T(8,128)S(1)} %fusion.50, bf16[8,32,256]{2,1,0:T(8,128)(2,1)} %reduce-scatter.3.cloned.1.call-done, bf16[64,256]{1,0:T(8,128)(2,1)S(1)} %copy-done.6), kind=kOutput, calls=%fused_computation.37 | convolution fusion | flops 50659328 | bytes 753664 | tf_op jit(solution)/shard_map/dot_general | solution.py:90
  96.7 0.3 fusion.63
  97.0 0.0 copy-start.3
  97.0 0.8 fusion.38
  97.9 0.1 copy-done.3
  97.9 0.9 convolution_convert_fusion.3
  (7 shorter events, 0.1 us)
Async XLA Ops:
  7.2 2.4 %copy-start = (bf16[8,32,64]{2,1,0:T(8,128)(2,1)S(1)}, bf16[8,32,64]{2,1,0:T(8,128)(2,1)}, u32[]{:S(2)}) copy-start(bf16[8,32,64]{2,1,0:T(8,128)(2,1)} %param.17) | copy-start | bytes 98308
  7.2 1.0 copy-start.1
  7.2 48.2 %reduce-scatter.5.cloned.1.call-start = ((), (), s32[]{:S(2)}) async-start(), calls=%async_computation.3 | async-start | bytes 294912 | tf_op jit(solution)/shard_map/reduce_scatter | solution.py:105
  8.2 0.8 copy-start.4
  8.4 0.7 copy-start.8
  9.4 0.8 copy-start.5
  10.1 0.8 copy-start.6
  24.2 0.9 copy-start.2
  24.2 71.3 %reduce-scatter.3.cloned.1.call-start = ((), (), s32[]{:S(2)}) async-start(), calls=%async_computation.2 | async-start | bytes 655360 | tf_op jit(solution)/shard_map/reduce_scatter | solution.py:78
  25.5 0.7 copy-start.9
  25.5 0.7 copy-start.10
  72.6 10.8 %copy-start.7 = (bf16[8,16,32]{2,0,1:T(8,128)(2,1)S(1)}, bf16[8,16,32]{2,0,1:T(8,128)(2,1)}, u32[]{:S(2)}) copy-start(bf16[8,16,32]{2,0,1:T(8,128)(2,1)} %reduce-scatter.5.cloned.1.call-done) | copy-start | bytes 24580
  97.0 0.9 copy-start.3
Sparse Core Ops, SparseCore 0:
  24.3 31.0 reduce-scatter.4
  72.1 23.4 reduce-scatter.2
where the time goes:
time: 106 us
  blocking collectives  45.3 us (43%)
  waiting for transfers between devices  30.1 us (28%)
  between operations  14.3 us (13%)
  local copies, waits for them, and re-layouts  6.44 us (6%)
  matrix products  5.12 us (5%)
  other arithmetic  4.33 us (4%)
    reduce_scatter x1, waiting for transfers between devices, per_device(): lax.psum_scatter(weight_part.astype(jnp.bfloat16), 'bulk', scatter_dimens...  19.7 us
    all_gather x1, blocking collectives, per_device(): weight_panel = lax.all_gather(weights_low, 'bulk', axis=1, tiled=True)  14.2 us
    all_gather x1, blocking collectives, per_device(): average_gradient = lax.all_gather(d_average_here, 'col', axis=1, tiled=True)  11.5 us
    psum x1, blocking collectives, per_device(): lax.psum(jnp.sum(weights_low.astype(jnp.float32) * d_weights, axis=2), 'c...  10.5 us
    reduce_scatter x1, waiting for transfers between devices, per_device(): lax.psum_scatter(partial_low, 'col', scatter_dimension=1, tiled=True)  10.4 us
    psum x1, blocking collectives, per_device(): totals = lax.psum(jnp.sum(exponent, axis=2), 'col')  9.09 us
    unnamed x22, local copies, waits for them, and re-layouts  3.31 us
  transfers between devices with their start and end apart: 2, of which 2 were waited for; matrix products, arithmetic and copies ran while one was open for 3% of the time, Pallas kernels for 0%

commit v1 on v0

--- a/solution.py
+++ b/solution.py
@@ -4,6 +4,12 @@
 from jax.sharding import PartitionSpec as P
 
 epsilon = 1e-05
+
+
+def stack_and_merge(value, mesh_axis, dim):
+    parts = lax.all_gather(value, mesh_axis, axis=0, tiled=False)
+    whole = jnp.concatenate(parts, axis=dim)
+    return whole
 
 
 def centred_sequences(inputs, scale_gain):
@@ -85,7 +91,7 @@
         residual_change_cotangent.astype(jnp.float32), out_wide.T, precision=finest_accuracy
     )
     d_average_here = (sigmoid_switch * d_gated).astype(jnp.bfloat16)
-    average_gradient = lax.all_gather(d_average_here, "col", axis=1, tiled=True)
+    average_gradient = stack_and_merge(d_average_here, "col", 1)
     switch_preimage_sensitivity = d_gated * pair_average * sigmoid_switch * (1.0 - sigmoid_switch)
     gate_contribution = jnp.dot(
         switch_preimage_sensitivity, switch_single_form.T, precision=finest_accuracy

time: 106 us -> 110 us (1.038)
  matrix products: 5.12 us -> 7.65 us
  waiting for transfers between devices: 30.1 us -> 31.6 us
    unnamed x22 -> x20, local copies, waits for them, and re-layouts: 3.31 us -> 0.06 us
    another operation x0 -> x2, local copies, waits for them, and re-layouts: none -> 2.4 us  [per_device(): average_gradient.reshape(device_sequences, all_tokens, number_of_heads, h...]
    reduce_scatter x1, waiting for transfers between devices: 19.7 us -> 21.2 us  [per_device(): lax.psum_scatter(weight_part.astype(jnp.bfloat16), 'bulk', scatter_dimens...]
where the time goes in v1:
time: 110 us; the launch traced here: 109 us
  blocking collectives  45.2 us (41%)
  waiting for transfers between devices  31.6 us (29%)
  between operations  14.4 us (13%)
  matrix products  7.65 us (7%)
  local copies, waits for them, and re-layouts  5.36 us (5%)
  other arithmetic  5.15 us (5%)
    reduce_scatter x1, waiting for transfers between devices, per_device(): lax.psum_scatter(weight_part.astype(jnp.bfloat16), 'bulk', scatter_dimens...  21.2 us
    all_gather x1, blocking collectives, per_device(): weight_panel = lax.all_gather(weights_low, 'bulk', axis=1, tiled=True)  14.2 us
    all_gather x1, blocking collectives, stack_and_merge(): parts = lax.all_gather(value, mesh_axis, axis=0, tiled=False)  11.5 us
    psum x1, blocking collectives, per_device(): lax.psum(jnp.sum(weights_low.astype(jnp.float32) * d_weights, axis=2), 'c...  10.4 us
    reduce_scatter x1, waiting for transfers between devices, per_device(): lax.psum_scatter(partial_low, 'col', scatter_dimension=1, tiled=True)  10.4 us
    psum x1, blocking collectives, per_device(): totals = lax.psum(jnp.sum(exponent, axis=2), 'col')  9.09 us
    another operation x2, local copies, waits for them, and re-layouts, per_device(): average_gradient.reshape(device_sequences, all_tokens, number_of_heads, h...  2.4 us
  transfers between devices with their start and end apart: 2, of which 2 were waited for; matrix products, arithmetic and copies ran while one was open for 3% of the time, Pallas kernels for 0%

profile of v1, /device:TPU:0, one launch (start us, length us, event | category | flops | bytes accessed | tf_op | source)
XLA Modules:
  0.0 109.4 jit_solution(8291395642825709479)
XLA Ops:
  7.2 0.0 copy-start
  7.2 0.0 reduce-scatter.5.cloned.1.call-start
  7.2 0.9 convert_reduce_fusion.1
  8.2 1.0 fusion.38
  9.2 0.0 copy-done
  9.2 0.9 fusion.49
  10.2 1.1 %multiply_convert_fusion = (bf16[8,32,256]{2,1,0:T(8,128)(2,1)S(1)}, f32[8,32,256]{2,1,0:T(8,128)S(1)}) fusion(f32[8,32,256]{2,1,0:T(8,128)S(1)} %fusion.49, bf16[64,256]{1,0:T(8,128)(2,1)} %param.14, bf16[8,32,64]{2,1,0:T(8,128)(2,1)} %param.9, f32[64]{0:T(128)} %param.11, f32[8,32]{1,0:T(8,128)S(1)} %add_rsqrt_fusion.1, ...), kind=kOutput, calls=%fused_computation.39 | convolution fusion | flops 8798208 | bytes 723200 | tf_op jit(solution)/shard_map/dot_general | solution.py:82
  11.3 11.5 %all-gather = bf16[32,32,256]{2,1,0:T(8,128)(2,1)S(1)} all-gather(bf16[8,32,256]{2,1,0:T(8,128)(2,1)S(1)} %get-tuple-element.9), channel_id=2, replica_groups=mesh['col'=4,'bulk'=8] {'col'}, dimensions={0}, use_global_device_ids=true | all-gather | bytes 655360 | tf_op jit(solution)/shard_map/all_gather | solution.py:10
  22.9 0.0 copy-start.1
  22.9 0.0 copy-start.3
  22.9 0.0 copy-start.7
  22.9 0.9 reshape_reshape.3
  23.8 0.0 copy-start.2
  23.8 1.5 %copy.59 = bf16[8,128,8,32]{1,3,0,2:T(8,128)(2,1)S(1)} copy(bf16[8,128,8,32]{3,2,1,0:T(8,128)(2,1)S(1)} %reshape_reshape.3) | data formatting | bytes 1048576 | tf_op jit(solution)/shard_map/reshape;reshape | solution.py:99
  25.3 0.0 copy-done.1
  25.3 0.0 copy-done.3
  25.3 0.0 copy-done.7
  25.4 0.0 copy-start.8
  25.4 0.0 copy-start.9
  25.4 0.3 convolution_convert_fusion.2
  25.6 0.2 reshape.60
  25.9 0.3 fusion.6
  26.2 0.9 copy.65
  27.1 0.0 reduce-scatter.5.cloned.1.call-update
  27.1 0.0 reduce-scatter.3.cloned.1.call-start
  27.2 0.0 copy-done.2
  27.2 0.1 convert_reduce_fusion
  27.3 0.3 fusion.20
  27.6 0.0 copy-done.8
  27.6 0.0 copy-done.9
  27.6 0.4 fusion.64
  28.1 9.1 %psum.14 = f32[8,16]{0,1:T(8,128)S(1)} all-reduce(f32[8,16]{0,1:T(8,128)S(1)} %get-tuple-element.11), channel_id=1, replica_groups=mesh['col'=4,'bulk'=8] {'col'}, use_global_device_ids=true, to_apply=%region_5.0 | all-reduce | flops 128 | bytes 1024 | tf_op jit(solution)/shard_map/psum | solution.py:62
  37.2 21.2 %reduce-scatter.5.cloned.1.call-done = bf16[8,16,32]{2,0,1:T(8,128)(2,1)} async-done(((bf16[8,128,32]{2,0,1:T(8,128)(2,1)}), bf16[8,16,32]{2,0,1:T(8,128)(2,1)}) %reduce-scatter.5.cloned.1.call-update) | async-done | bytes 8208 | tf_op jit(solution)/shard_map/reduce_scatter | solution.py:111
  58.4 0.9 fusion.44
  59.3 14.2 %all_gather.9 = bf16[8,128,32]{2,0,1:T(8,128)(2,1)S(1)} all-gather(bf16[8,16,32]{2,0,1:T(8,128)(2,1)S(1)} %get-tuple-element.8), channel_id=1, replica_groups=mesh['col'=4,'bulk'=8] {'bulk'}, dimensions={1}, use_global_device_ids=true | all-gather | bytes 73728 | tf_op jit(solution)/shard_map/all_gather | solution.py:65
  73.5 0.4 fusion
  73.9 0.0 copy-start.6
  73.9 1.0 copy.57
  74.9 0.0 reduce-scatter.3.cloned.1.call-update
  74.9 0.0 copy-start.5
  74.9 0.3 fusion.1
  75.2 0.3 copy.61
  75.6 0.0 copy-start.4
  75.6 0.4 convert_element_type.78
  76.0 10.4 %psum.15 = f32[8,16]{0,1:T(8,128)S(1)} all-reduce(f32[8,16]{0,1:T(8,128)S(1)} %get-tuple-element.7), channel_id=1, replica_groups=mesh['col'=4,'bulk'=8] {'col'}, use_global_device_ids=true, to_apply=%region_11.0 | all-reduce | flops 128 | bytes 1024 | tf_op jit(solution)/shard_map/psum | solution.py:114
  86.4 0.0 copy-done.6
  86.4 0.7 fusion.61
  87.1 1.0 fusion.19
  88.1 10.4 %reduce-scatter.3.cloned.1.call-done = bf16[8,32,256]{2,1,0:T(8,128)(2,1)} async-done(((bf16[8,128,256]{2,1,0:T(8,128)(2,1)}), bf16[8,32,256]{2,1,0:T(8,128)(2,1)}) %reduce-scatter.3.cloned.1.call-update) | async-done | bytes 131088 | tf_op jit(solution)/shard_map/reduce_scatter | solution.py:84
  98.4 0.0 copy-done.5
  98.4 1.2 %fusion.23 = f32[8,32,64]{2,1,0:T(8,128)S(1)} fusion(f32[8,32,256]{2,1,0:T(8,128)S(1)} %get-tuple-element.10, f32[8,32,256]{2,1,0:T(8,128)S(1)} %fusion.49, bf16[8,32,256]{2,1,0:T(8,128)(2,1)} %reduce-scatter.3.cloned.1.call-done, bf16[64,256]{1,0:T(8,128)(2,1)S(1)} %copy-done.5), kind=kOutput, calls=%fused_computation.37 | convolution fusion | flops 50659328 | bytes 753664 | tf_op jit(solution)/shard_map/dot_general | solution.py:96
  99.6 0.3 fusion.62
  99.9 0.8 fusion.37
  100.8 0.0 copy-done.4
  100.8 1.8 %convolution_convert_fusion.3 = bf16[8,32,64]{2,1,0:T(8,128)(2,1)} fusion(f32[8,32,256]{2,1,0:T(8,128)S(1)} %get-tuple-element.10, bf16[8,32,256]{2,1,0:T(8,128)(2,1)} %reduce-scatter.3.cloned.1.call-done, bf16[256,64]{0,1:T(8,128)(2,1)S(1)} %copy-done.4), kind=kOutput, calls=%fused_computation.14 | convolution fusion | flops 50479104 | bytes 458752 | tf_op jit(solution)/shard_map/dot_general | solution.py:87
  (8 shorter events, 0.1 us)
Async XLA Ops:
  7.2 2.1 %copy-start = (bf16[8,32,64]{2,1,0:T(8,128)(2,1)S(1)}, bf16[8,32,64]{2,1,0:T(8,128)(2,1)}, u32[]{:S(2)}) copy-start(bf16[8,32,64]{2,1,0:T(8,128)(2,1)} %param.17) | copy-start | bytes 98308
  7.2 51.2 %reduce-scatter.5.cloned.1.call-start = ((), (), s32[]{:S(2)}) async-start(), calls=%async_computation.3 | async-start | bytes 294912 | tf_op jit(solution)/shard_map/reduce_scatter | solution.py:111
  22.9 2.5 %copy-start.1 = (bf16[8,32,64]{2,1,0:T(8,128)(2,1)S(1)}, bf16[8,32,64]{2,1,0:T(8,128)(2,1)}, u32[]{:S(2)}) copy-start(bf16[8,32,64]{2,1,0:T(8,128)(2,1)} %param.9) | copy-start | bytes 98308
  22.9 2.5 %copy-start.3 = (bf16[64,256]{1,0:T(8,128)(2,1)S(1)}, bf16[64,256]{1,0:T(8,128)(2,1)}, u32[]{:S(2)}) copy-start(bf16[64,256]{1,0:T(8,128)(2,1)} %param.13) | copy-start | bytes 98308
  22.9 2.5 %copy-start.7 = (f32[64]{0:T(128)S(1)}, f32[64]{0:T(128)}, u32[]{:S(2)}) copy-start(f32[64]{0:T(128)} %param.11) | copy-start | bytes 772
  23.8 3.4 %copy-start.2 = (bf16[16,32,128]{2,1,0:T(8,128)(2,1)S(1)}, bf16[16,32,128]{2,1,0:T(8,128)(2,1)}, u32[]{:S(2)}) copy-start(bf16[16,32,128]{2,1,0:T(8,128)(2,1)} %param.10) | copy-start | bytes 393220
  25.4 2.3 %copy-start.8 = (bf16[128,8]{0,1:T(8,128)(2,1)S(1)}, bf16[128,8]{0,1:T(8,128)(2,1)}, u32[]{:S(2)}) copy-start(bf16[128,8]{0,1:T(8,128)(2,1)} %param.15) | copy-start | bytes 6148
  25.4 2.3 %copy-start.9 = (f32[128]{0:T(128)S(1)}, f32[128]{0:T(128)}, u32[]{:S(2)}) copy-start(f32[128]{0:T(128)} %param.12) | copy-start | bytes 1540
  27.1 71.3 %reduce-scatter.3.cloned.1.call-start = ((), (), s32[]{:S(2)}) async-start(), calls=%async_computation.2 | async-start | bytes 655360 | tf_op jit(solution)/shard_map/reduce_scatter | solution.py:84
  73.9 12.5 %copy-start.6 = (bf16[8,16,32]{2,0,1:T(8,128)(2,1)S(1)}, bf16[8,16,32]{2,0,1:T(8,128)(2,1)}, u32[]{:S(2)}) copy-start(bf16[8,16,32]{2,0,1:T(8,128)(2,1)} %reduce-scatter.5.cloned.1.call-done) | copy-start | bytes 24580
  74.9 23.5 %copy-start.5 = (bf16[64,256]{1,0:T(8,128)(2,1)S(1)}, bf16[64,256]{1,0:T(8,128)(2,1)}, u32[]{:S(2)}) copy-start(bf16[64,256]{1,0:T(8,128)(2,1)} %param.14) | copy-start | bytes 98308
  75.6 25.2 %copy-start.4 = (bf16[256,64]{0,1:T(8,128)(2,1)S(1)}, bf16[256,64]{0,1:T(8,128)(2,1)}, u32[]{:S(2)}) copy-start(bf16[256,64]{0,1:T(8,128)(2,1)} %param.16) | copy-start | bytes 98308
Sparse Core Ops, SparseCore 0:
  27.2 31.0 reduce-scatter.4
  75.0 23.3 reduce-scatter.2
